TPU v7x, 512 devices: a whole 4x4x16 slice. The times are simulated.
512 devices in a mesh: section: 8 (over y, x_hi), ctx: 16 (over z), dp: 4 (over x_lo, core).
Axes of the slice: x: 4 (x_hi: 2, x_lo: 2; x = x_hi * 2 + x_lo), y: 4, z: 16, core: 2. Of those that a mesh axis runs over, the one named last changes fastest.
Arguments:
- activations: bfloat16 [8, 4, 2048, 1280], P('section', 'dp', 'ctx'), may hold values from -6 to 6
- out_grads: bfloat16 [8, 4, 2048, 1280], P('section', 'dp', 'ctx'), may hold values from -6 to 6
- doc_ids: int32 [4, 16], replicated, may hold values from 0 to 3, never falling along the last dimension, each value on 1 to 12 neighbouring positions
- query_weight: bfloat16 [8, 1280, 640], P('section', None, 'dp'), may hold values from -0.195655948 to 0.195655948
- key_weight: bfloat16 [8, 1280, 640], P('section', None, 'dp'), may hold values from -3.0745935 to 3.0745935
- value_weight: bfloat16 [8, 1280, 640], P('section', None, 'dp'), may hold values from -0.15625 to 0.15625
- out_weight: bfloat16 [8, 640, 1280], P('section', 'dp'), may hold values from -0.25 to 0.25
Outputs:
- received_grad: bfloat16 [8, 4, 2048, 1280], P('section', 'dp', 'ctx')
Inputs may be any that keep to these rules, and one draw needn't show every extreme that they name: `doc_ids`: each page stack's documents are runs of whole blocks, numbered from 0 in order; a document covers at most 12 blocks.
All inputs are finite; a program needn't handle non-finite values.
Results may differ from a plain program's by a relative error of at most 0.0085.
The roundings to bfloat16 on the way count: a program that leaves them out, or rounds other values in their place, can miss the bound.
Values may be sent and summed in bfloat16 or wider, within the bound.
A program may use at most 128 MiB of HBM per device.

v0:
```python
import math

import jax
import jax.numpy as jnp
from jax import lax
from jax.sharding import PartitionSpec as P

HEAD_DIM = 80
BLOCK = 128


NEG = -1e30
HIGHEST = lax.Precision.HIGHEST


def from_behind(array, axis, by):
    length = lax.axis_size(axis)
    return lax.ppermute(array, axis, [(i, (i + by) % length) for i in range(length)])


def expand(allowed_blocks, query_len, key_len):
    page_count = allowed_blocks.shape[0]
    query_blocks = query_len // BLOCK
    key_blocks = key_len // BLOCK
    widened = jnp.broadcast_to(
        allowed_blocks[:, :, None, :, None], (page_count, query_blocks, BLOCK, key_blocks, BLOCK)
    )
    return widened.reshape(page_count, query_len, key_len)


def row_statistics(
    queries, out_grad, all_keys, all_values, block_table, my_offset, head_count, score_scale
):
    page_count, row_count, _ = queries.shape
    length = all_keys.shape[1]
    block_len = math.gcd(length, 512)
    query_four = queries.reshape(page_count, row_count, head_count, HEAD_DIM)
    grad_four = out_grad.reshape(page_count, row_count, head_count, HEAD_DIM)
    my_blocks = lax.dynamic_slice_in_dim(block_table, my_offset // BLOCK, row_count // BLOCK, 1)

    def row_visit(index, totals):
        key_offset = index * block_len
        key_block = lax.dynamic_slice_in_dim(all_keys, key_offset, block_len, 1).reshape(
            page_count, block_len, head_count, HEAD_DIM
        )
        value_block = lax.dynamic_slice_in_dim(all_values, key_offset, block_len, 1).reshape(
            page_count, block_len, head_count, HEAD_DIM
        )
        allowed = expand(
            lax.dynamic_slice_in_dim(my_blocks, key_offset // BLOCK, block_len // BLOCK, 2),
            row_count,
            block_len,
        )[:, None]
        old_max, old_sum, old_dot = totals
        scores = (
            jnp.einsum(
                "brhd,bkhd->bhrk",
                query_four,
                key_block,
                precision=HIGHEST,
                preferred_element_type=jnp.float32,
            )
            * score_scale
        )
        scores = jnp.where(allowed, scores, NEG)
        new_max = jnp.maximum(old_max, jnp.max(scores, axis=-1))
        weights = jnp.where(allowed, jnp.exp(scores - new_max[..., None]), 0.0)
        dprob = jnp.einsum(
            "brhd,bkhd->bhrk", grad_four, value_block, preferred_element_type=jnp.float32
        )
        factor = jnp.exp(old_max - new_max)
        return (
            new_max,
            old_sum * factor + jnp.sum(weights, axis=-1),
            old_dot * factor + jnp.sum(weights * dprob, axis=-1),
        )

    stat_shape = (page_count, head_count, row_count)
    zeros = jnp.zeros(stat_shape, jnp.float32)
    start_state = (jnp.full(stat_shape, NEG, jnp.float32), zeros, zeros)
    final_max, final_sum, final_dot = lax.fori_loop(0, length // block_len, row_visit, start_state)
    log_total = final_max + jnp.log(final_sum)
    row_delta = final_dot / final_sum
    return (jnp.transpose(log_total, (0, 2, 1)), jnp.transpose(row_delta, (0, 2, 1)))


def query_side(
    queries,
    out_grad,
    all_keys,
    all_values,
    block_table,
    my_offset,
    log_total,
    row_delta,
    head_count,
    score_scale,
):
    page_count, row_count, width = queries.shape
    length = all_keys.shape[1]
    block_len = math.gcd(length, 512)
    query_four = queries.reshape(page_count, row_count, head_count, HEAD_DIM)
    grad_four = out_grad.reshape(page_count, row_count, head_count, HEAD_DIM)
    log_heads = jnp.transpose(log_total, (0, 2, 1))
    delta_heads = jnp.transpose(row_delta, (0, 2, 1))
    my_blocks = lax.dynamic_slice_in_dim(block_table, my_offset // BLOCK, row_count // BLOCK, 1)

    def query_visit(index, totals):
        key_offset = index * block_len
        key_block = lax.dynamic_slice_in_dim(all_keys, key_offset, block_len, 1).reshape(
            page_count, block_len, head_count, HEAD_DIM
        )
        value_block = lax.dynamic_slice_in_dim(all_values, key_offset, block_len, 1).reshape(
            page_count, block_len, head_count, HEAD_DIM
        )
        allowed = expand(
            lax.dynamic_slice_in_dim(my_blocks, key_offset // BLOCK, block_len // BLOCK, 2),
            row_count,
            block_len,
        )[:, None]
        scores = (
            jnp.einsum(
                "brhd,bkhd->bhrk",
                query_four,
                key_block,
                precision=HIGHEST,
                preferred_element_type=jnp.float32,
            )
            * score_scale
        )
        scores = jnp.where(allowed, scores, NEG)
        prob = jnp.where(allowed, jnp.exp(scores - log_heads[..., None]), 0.0)
        dprob = jnp.einsum(
            "brhd,bkhd->bhrk", grad_four, value_block, preferred_element_type=jnp.float32
        )
        dscore = prob * (dprob - delta_heads[..., None])
        dscore_low = dscore.astype(jnp.bfloat16).astype(jnp.float32)
        return totals + jnp.einsum(
            "bhrk,bkhd->brhd",
            dscore_low,
            key_block,
            precision=HIGHEST,
            preferred_element_type=jnp.float32,
        )

    start_state = jnp.zeros((page_count, row_count, head_count, HEAD_DIM), jnp.float32)
    summed = lax.fori_loop(0, length // block_len, query_visit, start_state)
    return (summed * score_scale).astype(jnp.bfloat16).reshape(page_count, row_count, width)


def key_side(
    totals,
    portion,
    key_rows,
    value_rows,
    all_log_total,
    all_delta,
    block_table,
    my_offset,
    head_count,
    score_scale,
):
    part_queries, part_grads = portion
    page_count, part_len, _ = part_queries.shape
    row_count = key_rows.shape[1]
    block_len = math.gcd(part_len, 512)
    key_four = key_rows.reshape(page_count, row_count, head_count, HEAD_DIM)
    value_four = value_rows.reshape(page_count, row_count, head_count, HEAD_DIM)
    key_columns = lax.dynamic_slice_in_dim(block_table, my_offset // BLOCK, row_count // BLOCK, 2)

    def key_visit(index, state):
        query_offset = index * block_len
        query_part = lax.dynamic_slice_in_dim(part_queries, query_offset, block_len, 1).reshape(
            page_count, block_len, head_count, HEAD_DIM
        )
        grad_part = (
            lax.dynamic_slice_in_dim(part_grads, query_offset, block_len, 1)
            .astype(jnp.bfloat16)
            .reshape(page_count, block_len, head_count, HEAD_DIM)
        )
        log_part = jnp.transpose(
            lax.dynamic_slice_in_dim(all_log_total, query_offset, block_len, 1), (0, 2, 1)
        )
        delta_part = jnp.transpose(
            lax.dynamic_slice_in_dim(all_delta, query_offset, block_len, 1), (0, 2, 1)
        )
        allowed = expand(
            lax.dynamic_slice_in_dim(key_columns, query_offset // BLOCK, block_len // BLOCK, 1),
            block_len,
            row_count,
        )[:, None]
        key_total, value_total = state
        scores = (
            jnp.einsum(
                "bphd,brhd->bhpr",
                query_part,
                key_four,
                precision=HIGHEST,
                preferred_element_type=jnp.float32,
            )
            * score_scale
        )
        scores = jnp.where(allowed, scores, NEG)
        prob = jnp.where(allowed, jnp.exp(scores - log_part[..., None]), 0.0)
        value_total = value_total + jnp.einsum(
            "bhpr,bphd->brhd",
            prob.astype(jnp.bfloat16),
            grad_part,
            preferred_element_type=jnp.float32,
        )
        dprob = jnp.einsum(
            "bphd,brhd->bhpr", grad_part, value_four, preferred_element_type=jnp.float32
        )
        dscore = prob * (dprob - delta_part[..., None])
        dscore_low = dscore.astype(jnp.bfloat16).astype(jnp.float32)
        key_total = key_total + jnp.einsum(
            "bhpr,bphd->brhd",
            dscore_low,
            query_part,
            precision=HIGHEST,
            preferred_element_type=jnp.float32,
        )
        return (key_total, value_total)

    return lax.fori_loop(0, part_len // block_len, key_visit, totals)


def body(activations, out_grads, doc_ids, query_weight, key_weight, value_weight, out_weight):
    score_scale = HEAD_DIM ** (-0.5)
    row_count = activations.shape[2]
    my_offset = lax.axis_index("ctx") * row_count
    full_query, full_key, full_value, full_out = (
        lax.all_gather(query_weight, "dp", axis=2, tiled=True),
        lax.all_gather(key_weight, "dp", axis=2, tiled=True),
        lax.all_gather(value_weight, "dp", axis=2, tiled=True),
        lax.all_gather(out_weight, "dp", axis=1, tiled=True),
    )
    page_inputs = activations[0]
    page_upstream = out_grads[0]
    page_ids = lax.dynamic_slice_in_dim(doc_ids, lax.axis_index("dp"), 1, 0)
    proj_query = full_query[0]
    proj_key = full_key[0]
    proj_value = full_value[0]
    proj_out = full_out[0]
    head_count = proj_query.shape[1] // HEAD_DIM
    inputs = page_inputs.astype(jnp.float32)
    inv_rms = lax.rsqrt(jnp.mean(inputs * inputs, axis=-1, keepdims=True) + 1e-05)
    normed = (inputs * inv_rms).astype(jnp.bfloat16)
    queries = jnp.einsum("brd,dh->brh", normed, proj_query, preferred_element_type=jnp.float32)
    key_rows = jnp.einsum("brd,dh->brh", normed, proj_key, preferred_element_type=jnp.float32)
    value_rows = jnp.einsum(
        "brd,dh->brh", normed, proj_value, preferred_element_type=jnp.float32
    ).astype(jnp.bfloat16)
    out_grad = jnp.einsum(
        "brd,hd->brh", page_upstream, proj_out, preferred_element_type=jnp.float32
    ).astype(jnp.bfloat16)
    block_table = page_ids[:, :, None] == page_ids[:, None, :]
    all_keys, wide_values = (
        lax.all_gather(key_rows, "ctx", axis=1, tiled=True),
        lax.all_gather(value_rows.astype(jnp.float32), "ctx", axis=1, tiled=True),
    )
    all_values = wide_values.astype(jnp.bfloat16)
    log_total, row_delta = row_statistics(
        queries, out_grad, all_keys, all_values, block_table, my_offset, head_count, score_scale
    )
    all_log_total, all_delta = (
        lax.all_gather(log_total, "ctx", axis=1, tiled=True),
        lax.all_gather(row_delta, "ctx", axis=1, tiled=True),
    )
    q_grad = query_side(
        queries,
        out_grad,
        all_keys,
        all_values,
        block_table,
        my_offset,
        log_total,
        row_delta,
        head_count,
        score_scale,
    )
    empty = jnp.zeros((key_rows.shape[0], row_count, head_count, HEAD_DIM), jnp.float32)
    key_total, value_total = key_side(
        (empty, empty),
        (
            lax.all_gather(queries, "ctx", axis=1, tiled=True),
            lax.all_gather(out_grad.astype(jnp.float32), "ctx", axis=1, tiled=True),
        ),
        key_rows,
        value_rows,
        all_log_total,
        all_delta,
        block_table,
        my_offset,
        head_count,
        score_scale,
    )
    k_grad = (key_total * score_scale).astype(jnp.bfloat16).reshape(key_rows.shape)
    v_grad = value_total.astype(jnp.bfloat16).reshape(value_rows.shape)
    summed = jnp.einsum("brh,dh->brd", q_grad, proj_query, preferred_element_type=jnp.float32)
    summed = summed + jnp.einsum(
        "brh,dh->brd", k_grad, proj_key, preferred_element_type=jnp.float32
    )
    normed_grad = summed + jnp.einsum(
        "brh,dh->brd", v_grad, proj_value, preferred_element_type=jnp.float32
    )
    branch = inv_rms * normed_grad - inputs * inv_rms**3 * jnp.mean(
        normed_grad * inputs, axis=-1, keepdims=True
    )
    branch_grad = branch.astype(jnp.bfloat16)[None]
    return from_behind(branch_grad, "section", -1)


def solution(mesh):
    return jax.shard_map(
        body,
        mesh=mesh,
        in_specs=(
            P("section", "dp", "ctx", None),
            P("section", "dp", "ctx", None),
            P(),
            P("section", None, "dp"),
            P("section", None, "dp"),
            P("section", None, "dp"),
            P("section", "dp", None),
        ),
        out_specs=P("section", "dp", "ctx", None),
        check_vma=False,
    )
```

profile of v0, /device:TPU:30, one launch (start us, length us, event | category | flops | bytes accessed | tf_op | source)
XLA Modules:
  0.0 580.5 jit_solution(2038924234252000097)
XLA Ops:
  10.5 35.4 %all-gather.17.cloned.1.call-done = bf16[1,1280,640]{1,2,0:T(8,128)(2,1)} async-done(((bf16[1,1280,160]{1,2,0:T(8,128)(2,1)}), bf16[1,1280,640]{1,2,0:T(8,128)(2,1)}) %all-gather.17.cloned.1.call-update) | async-done | bytes 1638416 | tf_op jit(solution)/shard_map/all_gather | solution.py:235
  48.8 33.3 %all-gather.13.cloned.1.call-done = bf16[1,1280,640]{1,2,0:T(8,128)(2,1)} async-done(((bf16[1,1280,160]{1,2,0:T(8,128)(2,1)}), bf16[1,1280,640]{1,2,0:T(8,128)(2,1)}) %all-gather.13.cloned.1.call-update) | async-done | bytes 1638416 | tf_op jit(solution)/shard_map/all_gather | solution.py:234
  84.9 33.2 %all-gather.19.cloned.1.call-done = bf16[1,640,1280]{2,1,0:T(8,128)(2,1)} async-done(((bf16[1,160,1280]{2,1,0:T(8,128)(2,1)}), bf16[1,640,1280]{2,1,0:T(8,128)(2,1)}) %all-gather.19.cloned.1.call-update) | async-done | bytes 1638416 | tf_op jit(solution)/shard_map/all_gather | solution.py:236
  125.3 28.9 %all-gather.15.cloned.1.call-done = bf16[1,1280,640]{1,2,0:T(8,128)(2,1)} async-done(((bf16[1,1280,160]{1,2,0:T(8,128)(2,1)}), bf16[1,1280,640]{1,2,0:T(8,128)(2,1)}) %all-gather.15.cloned.1.call-update) | async-done | bytes 1638416 | tf_op jit(solution)/shard_map/all_gather | solution.py:233
  158.5 74.3 %all-gather.23.cloned.1.call-done = bf16[2048,640]{1,0:T(8,128)(2,1)} async-done(((bf16[128,640]{1,0:T(8,128)(2,1)}), bf16[2048,640]{1,0:T(8,128)(2,1)}) %all-gather.23.cloned.1.call-update) | async-done | bytes 2621456 | tf_op jit(solution)/shard_map/all_gather | solution.py:260
  232.8 4.5 copy.22
  237.2 75.2 %all-gather.21.cloned.1.call-done = f32[2048,640]{1,0:T(8,128)} async-done(((f32[128,640]{1,0:T(8,128)}), f32[2048,640]{1,0:T(8,128)}) %all-gather.21.cloned.1.call-update) | async-done | bytes 5242896 | tf_op jit(solution)/shard_map/all_gather | solution.py:259
  312.5 6.0 %copy.23 = f32[1,2048,640]{1,2,0:T(8,128)} copy(f32[1,2048,640]{2,1,0:T(8,128)} %bitcast.272) | data formatting | bytes 10485760
  318.5 42.2 %while.54 = (s32[]{:T(128)}, f32[1,8,128]{2,1,0:T(8,128)S(1)}, f32[1,8,128]{2,1,0:T(8,128)S(1)}, f32[1,8,128]{2,1,0:T(8,128)S(1)}, pred[1,1,16]{2,1,0:T(4,128)(4...) while((s32[]{:T(128)}, f32[1,8,128]{2,1,0:T(8,128)S(1)}, ...), condition=%wide.region_5.6_spmd.clone, body=%wide.region_1.5_spmd.clone.sunk | while | flops 594549760 | bytes 12757413 | solution.py:81
  322.7 3.6 bitcast_reduce_fusion.2
  343.8 3.6 bitcast_reduce_fusion.2
  360.7 30.7 %all_gather.37 = f32[1,2048,8]{1,2,0:T(8,128)} all-gather(f32[1,128,8]{1,2,0:T(8,128)S(1)} %bitcast.287), channel_id=1, replica_groups=mesh['section'=8,'ctx'=16,'dp'=4] {'ctx'}, dimensions={1}, use_global_device_ids=true | all-gather | bytes 69632 | tf_op jit(solution)/shard_map/all_gather | solution.py:267
  391.4 28.8 %all_gather.39 = f32[1,2048,8]{1,2,0:T(8,128)} all-gather(f32[1,128,8]{1,2,0:T(8,128)S(1)} %bitcast.285), channel_id=1, replica_groups=mesh['section'=8,'ctx'=16,'dp'=4] {'ctx'}, dimensions={1}, use_global_device_ids=true | all-gather | bytes 69632 | tf_op jit(solution)/shard_map/all_gather | solution.py:268
  420.1 56.8 %while.55 = (s32[]{:T(128)}, f32[1,128,8,80]{1,3,2,0:T(8,128)}, f32[1,2048,640]{1,2,0:T(8,128)}, pred[1,1,16]{2,1,0:T(4,128)(4,1)}, f32[1,128,8,80]{3,2,1,0:T(8,...) while((s32[]{:T(128)}, f32[1,128,8,80]{1,3,2,0:T(8,128)}, ...), condition=%wide.region_7.8_spmd.clone, body=%wide.region_6.7_spmd.clone.sunk | while | flops 1094352896 | bytes 14656932 | solution.py:147
  421.6 4.8 fusion.99
  435.1 4.8 fusion.99
  449.5 4.8 fusion.99
  463.9 4.8 fusion.99
  478.6 76.3 %while.56 = (s32[]{:T(128)}, f32[1,128,8,80]{1,3,2,0:T(8,128)S(1)}, f32[1,128,8,80]{1,3,2,0:T(8,128)}, f32[1,2048,640]{2,1,0:T(8,128)}, pred[1,16,1]{1,2,0:T(4,1...) while((s32[]{:T(128)}, f32[1,128,8,80]{1,3,2,0:T(8,128)S(1)}, ...), condition=%wide.region_9.10_spmd.clone, body=%wide.region_8.9_spmd.clone.sunk | while | flops 1178927104 | bytes 26019420 | solution.py:225
  482.4 5.4 exponential_select_fusion.2
  501.5 5.4 exponential_select_fusion.2
  520.6 5.4 exponential_select_fusion.2
  539.7 5.4 exponential_select_fusion.2
  563.7 9.2 %collective-permute-done = bf16[1,1,128,1280]{3,2,1,0:T(8,128)(2,1)S(1)} collective-permute-done((bf16[1,1,128,1280]{3,2,1,0:T(8,128)(2,1)S(1)}, bf16[1,1,128,1280]{3,2,1,0:T(8,128)(2,1)S(1)}, u32[]{:S(2)}, u32[]{:S(2)}) %collective-permute-start) | collective-permute-done | bytes 327712 | tf_op jit(solution)/shard_map/ppermute | solution.py:18
  (205 shorter events, 158.7 us)
Async XLA Ops:
  6.5 111.7 %copy-start = (bf16[1,1,128,1280]{3,2,1,0:T(8,128)(2,1)S(1)}, bf16[1,1,128,1280]{3,2,1,0:T(8,128)(2,1)}, u32[]{:S(2)}) copy-start(bf16[1,1,128,1280]{3,2,1,0:T(8,128)(2,1)} %param.14) | copy-start | bytes 983044
  6.5 39.4 %copy-start.2 = (bf16[1,1,128,1280]{3,2,1,0:T(8,128)(2,1)S(1)}, bf16[1,1,128,1280]{3,2,1,0:T(8,128)(2,1)}, u32[]{:S(2)}) copy-start(bf16[1,1,128,1280]{3,2,1,0:T(8,128)(2,1)} %param.13) | copy-start | bytes 983044
  6.5 39.4 %all-gather.17.cloned.1.call-start = ((), (), s32[]{:S(2)}) async-start(), calls=%async_computation.2 | async-start | bytes 2048000 | tf_op jit(solution)/shard_map/all_gather | solution.py:235
  7.3 74.8 %all-gather.13.cloned.1.call-start = ((), (), s32[]{:S(2)}) async-start(), calls=%async_computation | async-start | bytes 2048000 | tf_op jit(solution)/shard_map/all_gather | solution.py:234
  8.0 110.2 %all-gather.19.cloned.1.call-start = ((), (), s32[]{:S(2)}) async-start(), calls=%async_computation.3 | async-start | bytes 2048000 | tf_op jit(solution)/shard_map/all_gather | solution.py:236
  8.7 145.4 %all-gather.15.cloned.1.call-start = ((), (), s32[]{:S(2)}) async-start(), calls=%async_computation.1 | async-start | bytes 2048000 | tf_op jit(solution)/shard_map/all_gather | solution.py:233
  9.3 223.4 %all-gather.23.cloned.1.call-start = ((), (), s32[]{:S(2)}) async-start(), calls=%async_computation.5 | async-start | bytes 2785280 | tf_op jit(solution)/shard_map/all_gather | solution.py:260
  48.7 263.8 %all-gather.21.cloned.1.call-start = ((), (), s32[]{:S(2)}) async-start(), calls=%async_computation.4 | async-start | bytes 5570560 | tf_op jit(solution)/shard_map/all_gather | solution.py:259
  84.9 39.3 %copy-start.9 = (f32[128,640]{1,0:T(8,128)S(1)}, f32[128,640]{1,0:T(8,128)}, u32[]{:S(2)}) copy-start(f32[128,640]{1,0:T(8,128)} %fusion.26) | copy-start | bytes 983044
  84.9 40.3 %copy-start.10 = (bf16[128,640]{1,0:T(8,128)(2,1)S(1)}, bf16[128,640]{1,0:T(8,128)(2,1)}, u32[]{:S(2)}) copy-start(bf16[128,640]{1,0:T(8,128)(2,1)} %fusion.28) | copy-start | bytes 491524
  84.9 393.7 %all-gather.27.cloned.1.call-start = ((), (), s32[]{:S(2)}) async-start(), calls=%async_computation.7 | async-start | bytes 2785280 | tf_op jit(solution)/shard_map/all_gather | solution.py:287
  120.9 357.6 %all-gather.25.cloned.1.call-start = ((), (), s32[]{:S(2)}) async-start(), calls=%async_computation.6 | async-start | bytes 5570560 | tf_op jit(solution)/shard_map/all_gather | solution.py:286
  420.1 58.5 %copy-start.1 = (f32[1,128,8,80]{1,3,2,0:T(8,128)S(1)}, f32[1,128,8,80]{1,3,2,0:T(8,128)}, u32[]{:S(2)}) copy-start(f32[1,128,8,80]{1,3,2,0:T(8,128)} %custom-call.4) | copy-start | bytes 983044
  478.6 3.7 copy-start.12
  478.6 3.8 copy-start.11
  494.0 2.5 copy-start.4
  497.7 3.7 copy-start.12
  497.7 3.8 copy-start.11
  516.8 3.7 copy-start.12
  516.8 3.8 copy-start.11
  535.8 3.7 copy-start.12
  535.8 3.8 copy-start.11
  554.9 3.2 copy-start.7
  560.4 12.6 %collective-permute-start = (bf16[1,1,128,1280]{3,2,1,0:T(8,128)(2,1)S(1)}, bf16[1,1,128,1280]{3,2,1,0:T(8,128)(2,1)S(1)}, u32[]{:S(2)}, u32[]{:S(2)}) collective-permute-start(bf16[1,1,128,1280]{3,2,1,0:T(8,128)(2,1)S(1)} %fusion.44), channel_id=1, source_target_pairs={{0,448},{64,0},{128,64},{192,128},{256,192},{320,256},{384,320},{4... | collective-permute-start | bytes 983048 | tf_op jit(solution)/shard_map/ppermute | solution.py:18
  (10 other events, 14.3 us)
Sparse Core Ops, SparseCore 0:
  9.5 36.4 all-gather.16
  48.0 33.9 all-gather.12
  84.2 33.9 all-gather.18
  120.1 33.9 all-gather.14
  156.1 76.6 all-gather.22
  234.7 77.7 all-gather.20
  314.5 70.9 all-gather.26
  387.6 78.0 all-gather.24
where the time goes:
time: 583 us; the launch traced here: 581 us
  waiting for transfers between devices  292 us (50%)
  matrix products  120 us (21%)
  local copies, waits for them, and re-layouts  83.9 us (14%)
  blocking collectives  59.4 us (10%)
  between operations  13.7 us (2%)
  other arithmetic  6.74 us (1%)
    all_gather x1, waiting for transfers between devices, body(): lax.all_gather(key_rows, 'ctx', axis=1, tiled=True)  75.2 us
    all_gather x1, waiting for transfers between devices, body(): lax.all_gather(value_rows.astype(jnp.float32), 'ctx', axis=1, tiled=True)  74.3 us
    all_gather x1, waiting for transfers between devices, body(): lax.all_gather(value_weight, 'dp', axis=2, tiled=True)  35.4 us
    all_gather x1, waiting for transfers between devices, body(): lax.all_gather(key_weight, 'dp', axis=2, tiled=True)  33.3 us
    all_gather x1, waiting for transfers between devices, body(): lax.all_gather(out_weight, 'dp', axis=1, tiled=True)  33.2 us
    all_gather x1, blocking collectives, body(): lax.all_gather(log_total, 'ctx', axis=1, tiled=True)  30.7 us
    all_gather x1, waiting for transfers between devices, body(): lax.all_gather(query_weight, 'dp', axis=2, tiled=True)  28.9 us
    all_gather x1, blocking collectives, body(): lax.all_gather(row_delta, 'ctx', axis=1, tiled=True)  28.8 us
  transfers between devices with their start and end apart: 9, of which 7 were waited for; matrix products, arithmetic and copies ran while one was open for 22% of the time, Pallas kernels for 0%

commit v1 on v0

v1 whole, which is shorter than its diff:
```python
import functools

import jax
import jax.numpy as jnp
from jax import lax
from jax.experimental import pallas as pl
from jax.experimental.pallas import tpu as pltpu
from jax.sharding import PartitionSpec as P

HEAD_DIM = 80
BLOCK = 128
WIDTH = 1280
N_CTX = 16
HALF = 8
SCALE = HEAD_DIM ** (-0.5)
NEG = -1e30
H1, H2, H3, H4, H6 = (n * HEAD_DIM for n in (1, 2, 3, 4, 6))
F32 = jnp.float32
BF16 = jnp.bfloat16
NT = (((1,), (1,)), ((), ()))


def dot(a, b):
    return jnp.dot(a, b, preferred_element_type=F32)


def dot_nt(a, b):
    return lax.dot_general(a, b, NT, preferred_element_type=F32)


def flip(matrix):
    return matrix.astype(F32).T.astype(BF16)


def split(wide):
    high = wide.astype(BF16)
    return high, (wide - high.astype(F32)).astype(BF16)


def kernel(
    docs_ref,
    doc_row_ref,
    x_ref,
    og_ref,
    w_ref,
    out_ref,
    weights,
    normed,
    send,
    recv,
    kv_other,
    keys3,
    values,
    kv_grad,
    kv_partial,
    back_q,
    back_kv,
    got_q,
    got_kv,
    total,
    branch_out,
    w_send,
    relay_send,
    w_recv,
    send_sem,
    recv_sem,
    kv_send,
    kv_recv,
    part_send,
    part_recv,
    bq_send,
    bq_recv,
    bkv_send,
    bkv_recv,
    out_send,
    out_recv,
):
    section = lax.axis_index("section")
    n_section = lax.axis_size("section")
    z = lax.axis_index("ctx")
    dp = lax.axis_index("dp")
    x, c = dp // 2, dp % 2
    z_half, z_low = z // HALF, z % HALF
    core_peer = {"dp": 2 * x + 1 - c}
    x_peer = {"dp": 2 * (1 - x) + c}
    before = {"section": (section + n_section - 1) % n_section}
    after = {"section": (section + 1) % n_section}
    alone = z_half == c

    def peer(index):
        return {"ctx": HALF * c + index, "dp": 2 * x + z_half}

    barrier = pltpu.get_barrier_semaphore()
    for other in (core_peer, x_peer, before, after):
        pl.semaphore_signal(barrier, inc=1, device_id=other)

    def greet(index, carry):
        @pl.when(jnp.logical_not(alone & (index == z_low)))
        def _():
            pl.semaphore_signal(barrier, inc=1, device_id=peer(index))

        return carry

    lax.fori_loop(0, HALF, greet, 0)

    def weight_slot(r, j):
        return 4 * j + 2 * ((x + r // 2) % 2) + (c + r % 2) % 2

    def own_weights(j):
        return pltpu.make_async_copy(w_ref.at[j], weights.at[weight_slot(0, j)], w_recv.at[0, j])

    def pass_weights(r, j, target, send_sem_ref, arrive_r):
        block = weights.at[weight_slot(r, j)]
        return pltpu.make_async_remote_copy(
            src_ref=block,
            dst_ref=block,
            send_sem=send_sem_ref,
            recv_sem=w_recv.at[arrive_r, j],
            device_id=target,
        )

    def to_x(j):
        return pass_weights(0, j, x_peer, w_send.at[0, j], 2)

    def to_core(j):
        return pass_weights(0, j, core_peer, w_send.at[1, j], 1)

    def relay(j):
        return pass_weights(2, j, core_peer, relay_send.at[j], 3)

    def weights_here(r, j):
        block = weights.at[weight_slot(r, j)]
        pltpu.make_async_copy(block, block, w_recv.at[r, j]).wait()

    for j in range(2):
        own_weights(j).start()

    inputs = x_ref[...].astype(F32)
    inv_rms = lax.rsqrt(jnp.mean(inputs * inputs, axis=-1, keepdims=True) + 1e-05)
    normed[...] = (inputs * inv_rms).astype(BF16)

    own_weights(0).wait()
    own_weights(1).wait()
    pl.semaphore_wait(barrier, 12 - alone.astype(jnp.int32))
    for j in range(2):
        to_x(j).start()
    for j in range(2):
        to_core(j).start()

    def send_copy(index):
        return pltpu.make_async_remote_copy(
            src_ref=send.at[index],
            dst_ref=recv.at[z_low],
            send_sem=send_sem.at[index],
            recv_sem=recv_sem.at[z_low],
            device_id=peer(index),
        )

    def project(slot):
        w = weights.at[slot]
        qkv = dot_nt(w[0:H3], normed[...])
        out_grad = dot_nt(w[H3:H4], og_ref[...])
        q_high, q_low = split(qkv[0:H1])
        k_high, k_low = split(qkv[H1:H2])
        message = send.at[slot]
        message[0:H1] = q_high
        message[H1:H2] = q_low
        message[H2:H3] = out_grad.astype(BF16)
        message[H3:H4] = k_high
        message[H4 : H4 + H1] = k_low
        message[H4 + H1 : H6] = qkv[H2:H3].astype(BF16)
        mine = alone & (slot == z_low)

        @pl.when(mine)
        def _():
            pltpu.make_async_copy(message, recv.at[z_low], recv_sem.at[z_low]).start()

        @pl.when(jnp.logical_not(mine))
        def _():
            send_copy(slot).start()

    def near(t, carry):
        r, j = t // 2, t % 2

        @pl.when(r == 1)
        def _():
            weights_here(1, j)

        project(weight_slot(r, j))
        return carry

    lax.fori_loop(0, 4, near, 0)

    def far(t, carry):
        r, j = 2 + t % 2, t // 2
        weights_here(r, j)

        @pl.when(r == 2)
        def _():
            relay(j).start()

        project(weight_slot(r, j))
        return carry

    lax.fori_loop(0, 4, far, 0)

    def kv_copy(index):
        return pltpu.make_async_remote_copy(
            src_ref=recv.at[index, pl.ds(H3, H3)],
            dst_ref=kv_other.at[index],
            send_sem=kv_send.at[index],
            recv_sem=kv_recv.at[index],
            device_id=core_peer,
        )

    def place(block, kv):
        lanes = pl.ds(pl.multiple_of(block * BLOCK, BLOCK), BLOCK)
        keys3[0:H2, lanes] = kv[0:H2]
        keys3[H2:H3, lanes] = kv[0:H1]
        values[:, lanes] = kv[H2:H3]

    def arrive(index, carry):
        block = recv.at[index]
        pltpu.make_async_copy(block, block, recv_sem.at[index]).wait()
        kv_copy(index).start()
        place(HALF * c + index, recv[index, H3:H6])
        return carry

    lax.fori_loop(0, HALF, arrive, 0)

    def arrive_other(index, carry):
        kv_copy(index).wait_recv()
        place(HALF * (1 - c) + index, kv_other[index])
        return carry

    lax.fori_loop(0, HALF, arrive_other, 0)

    page = 2 * x + z_half
    doc_row = doc_row_ref[page]
    kv_grad[...] = jnp.zeros_like(kv_grad)

    def return_q(index):
        return pltpu.make_async_remote_copy(
            src_ref=back_q.at[index],
            dst_ref=got_q.at[z_low],
            send_sem=bq_send.at[index],
            recv_sem=bq_recv.at[z_low],
            device_id=peer_back(index),
        )

    def return_kv(index):
        return pltpu.make_async_remote_copy(
            src_ref=back_kv.at[index],
            dst_ref=got_kv.at[z_low],
            send_sem=bkv_send.at[index],
            recv_sem=bkv_recv.at[z_low],
            device_id=peer_back(index),
        )

    def peer_back(index):
        return peer(index)

    def attend(chunk, carry):
        one, two = recv.at[2 * chunk], recv.at[2 * chunk + 1]
        q_pair = jnp.concatenate([one[0:H2], two[0:H2]], axis=1)
        g_flat = jnp.concatenate([one[H2:H3], two[H2:H3]], axis=1)
        q3 = flip(jnp.concatenate([q_pair[0:H1], q_pair], axis=0))
        g = flip(g_flat)
        first = docs_ref[page, HALF * c + 2 * chunk]
        second = docs_ref[page, HALF * c + 2 * chunk + 1]
        rows = lax.broadcasted_iota(jnp.int32, (2 * BLOCK, 1), 0)
        allowed = jnp.where(rows < BLOCK, first, second) == doc_row
        scores = jnp.where(allowed, dot(q3, keys3[...]) * SCALE, NEG)
        top = jnp.max(scores, axis=-1, keepdims=True)
        weight = jnp.exp(scores - top)
        share = 1.0 / jnp.sum(weight, axis=-1, keepdims=True)
        prob = weight * share
        dprob = dot(g, values[...])
        delta = jnp.sum(prob * dprob, axis=-1, keepdims=True)
        dscore = (prob * (dprob - delta)).astype(BF16)
        q_grad = dot_nt(keys3[0:H2], dscore)
        q_grad = ((q_grad[0:H1] + q_grad[H1:H2]) * SCALE).astype(BF16)
        back_q[2 * chunk] = q_grad[:, 0:BLOCK]
        back_q[2 * chunk + 1] = q_grad[:, BLOCK:]
        k_grad = dot(q_pair, dscore)
        kv_grad[0:H1] += (k_grad[0:H1] + k_grad[H1:H2]) * SCALE
        kv_grad[H1:H2] += dot(g_flat, prob.astype(BF16))
        for side in range(2):
            index = 2 * chunk + side
            mine = alone & (index == z_low)

            @pl.when(mine)
            def _():
                pltpu.make_async_copy(
                    back_q.at[index], got_q.at[z_low], bq_recv.at[z_low]
                ).start()

            @pl.when(jnp.logical_not(mine))
            def _():
                return_q(index).start()

        return carry

    lax.fori_loop(0, HALF // 2, attend, 0)

    def half_lanes(core):
        return pl.ds(pl.multiple_of(core * HALF * BLOCK, BLOCK), HALF * BLOCK)

    partial = pltpu.make_async_remote_copy(
        src_ref=kv_grad.at[:, half_lanes(1 - c)],
        dst_ref=kv_partial,
        send_sem=part_send,
        recv_sem=part_recv,
        device_id=core_peer,
    )
    partial.start()
    partial.wait_recv()

    def finish_kv(index, carry):
        mine_lanes = pl.ds(pl.multiple_of((HALF * c + index) * BLOCK, BLOCK), BLOCK)
        lanes = pl.ds(pl.multiple_of(index * BLOCK, BLOCK), BLOCK)
        back_kv[index] = (kv_grad[:, mine_lanes] + kv_partial[:, lanes]).astype(BF16)
        mine = alone & (index == z_low)

        @pl.when(mine)
        def _():
            pltpu.make_async_copy(
                back_kv.at[index], got_kv.at[z_low], bkv_recv.at[z_low]
            ).start()

        @pl.when(jnp.logical_not(mine))
        def _():
            return_kv(index).start()

        return carry

    lax.fori_loop(0, HALF, finish_kv, 0)

    total[...] = jnp.zeros_like(total)

    def combine(index, carry):
        q_block, kv_block = got_q.at[index], got_kv.at[index]
        pltpu.make_async_copy(q_block, q_block, bq_recv.at[index]).wait()
        pltpu.make_async_copy(kv_block, kv_block, bkv_recv.at[index]).wait()
        grads = jnp.concatenate([q_block[...], kv_block[...]], axis=0)
        total[...] += dot(flip(grads), weights[index, 0:H3])
        return carry

    lax.fori_loop(0, HALF, combine, 0)

    again = x_ref[...].astype(F32)
    rms = lax.rsqrt(jnp.mean(again * again, axis=-1, keepdims=True) + 1e-05)
    grad = total[...]
    branch_out[...] = (
        rms * grad - again * rms**3 * jnp.mean(grad * again, axis=-1, keepdims=True)
    ).astype(BF16)
    shift = pltpu.make_async_remote_copy(
        src_ref=branch_out,
        dst_ref=out_ref,
        send_sem=out_send,
        recv_sem=out_recv,
        device_id=before,
    )
    shift.start()

    for j in range(2):
        to_x(j).wait_send()
        to_core(j).wait_send()
        relay(j).wait_send()
    partial.wait_send()

    def drain(index, carry):
        kv_copy(index).wait_send()

        @pl.when(jnp.logical_not(alone & (index == z_low)))
        def _():
            send_copy(index).wait_send()
            return_q(index).wait_send()
            return_kv(index).wait_send()

        return carry

    lax.fori_loop(0, HALF, drain, 0)
    shift.wait()


def body(activations, out_grads, doc_ids, query_weight, key_weight, value_weight, out_weight):
    tokens = activations.shape[2]

    def by_head(weight):
        return weight[0].T.reshape(2, HEAD_DIM, WIDTH)

    weights = jnp.concatenate(
        [
            by_head(query_weight),
            by_head(key_weight),
            by_head(value_weight),
            out_weight[0].reshape(2, HEAD_DIM, WIDTH),
        ],
        axis=1,
    )
    doc_row = jnp.repeat(doc_ids, BLOCK, axis=1)[:, None, :]
    vmem = pl.BlockSpec(memory_space=pltpu.VMEM)
    dma = pltpu.SemaphoreType.DMA
    out = pl.pallas_call(
        kernel,
        out_shape=jax.ShapeDtypeStruct((tokens, WIDTH), BF16),
        in_specs=[
            pl.BlockSpec(memory_space=pltpu.SMEM),
            vmem,
            vmem,
            vmem,
            pl.BlockSpec(memory_space=pl.ANY),
        ],
        out_specs=vmem,
        scratch_shapes=[
            pltpu.VMEM((HALF, H4, WIDTH), BF16),
            pltpu.VMEM((BLOCK, WIDTH), BF16),
            pltpu.VMEM((HALF, H6, BLOCK), BF16),
            pltpu.VMEM((HALF, H6, BLOCK), BF16),
            pltpu.VMEM((HALF, H3, BLOCK), BF16),
            pltpu.VMEM((H3, N_CTX * BLOCK), BF16),
            pltpu.VMEM((H1, N_CTX * BLOCK), BF16),
            pltpu.VMEM((H2, N_CTX * BLOCK), F32),
            pltpu.VMEM((H2, HALF * BLOCK), F32),
            pltpu.VMEM((HALF, H1, BLOCK), BF16),
            pltpu.VMEM((HALF, H2, BLOCK), BF16),
            pltpu.VMEM((HALF, H1, BLOCK), BF16),
            pltpu.VMEM((HALF, H2, BLOCK), BF16),
            pltpu.VMEM((BLOCK, WIDTH), F32),
            pltpu.VMEM((BLOCK, WIDTH), BF16),
            dma((2, 2)),
            dma((2,)),
            dma((4, 2)),
            dma((HALF,)),
            dma((HALF,)),
            dma((HALF,)),
            dma((HALF,)),
            dma,
            dma,
            dma((HALF,)),
            dma((HALF,)),
            dma((HALF,)),
            dma((HALF,)),
            dma,
            dma,
        ],
        compiler_params=pltpu.CompilerParams(
            collective_id=0, has_side_effects=True, vmem_limit_bytes=48 * 2**20
        ),
    )(doc_ids, doc_row, activations[0, 0], out_grads[0, 0], weights)
    return out[None, None]


def solution(mesh):
    return jax.shard_map(
        body,
        mesh=mesh,
        in_specs=(
            P("section", "dp", "ctx", None),
            P("section", "dp", "ctx", None),
            P(),
            P("section", None, "dp"),
            P("section", None, "dp"),
            P("section", None, "dp"),
            P("section", "dp", None),
        ),
        out_specs=P("section", "dp", "ctx", None),
        check_vma=False,
    )
```

time: 583 us -> 116 us (0.20)
  the two profiles are of different devices: /device:TPU:30 before, /device:TPU:159 now
where the time goes in v1:
time: 116 us
  Pallas kernels  113 us (97%)
  other arithmetic  1.55 us (1%)
  local copies, waits for them, and re-layouts  1.49 us (1%)
    pallas_call x1, Pallas kernels, body(): pl.pallas_call(kernel, out_shape=jax.ShapeDtypeStruct((tokens, WIDTH), BF...  113 us

profile of v1, /device:TPU:159, one launch (start us, length us, event | category | flops | bytes accessed | tf_op | source)
XLA Modules:
  0.0 116.2 jit_solution(11635112935138376837)
XLA Ops:
  0.0 0.8 broadcast_in_dim.6
  0.8 0.0 copy-start
  0.8 0.0 copy-start.1
  0.8 0.0 copy-start.2
  0.8 1.5 %pad_maximum_fusion.w_ref = bf16[2,320,1280]{2,1,0:T(8,128)(2,1)S(1)} fusion(bf16[2,80,1280]{2,1,0:T(8,128)(2,1)} %bitcast.24, bf16[2,80,1280]{2,1,0:T(8,128)(2,1)} %bitcast.25, bf16[2,80,1280]{2,1,0:T(8,128)(2,1)} %bitcast.26, bf16[2,80,1280]{2,1,0:T(8,128)(2,1)} %bitcast.27), kind=kLoop, calls=%fused_computation | loop fusion | flops 6553600 | bytes 3276800 | tf_op jit(solution)/shard_map/concatenate | solution.py:393
  2.3 0.0 copy-done
  2.3 0.0 copy-done.1
  2.3 0.0 copy-done.2
  2.3 113.1 %shard_map.73 = bf16[128,1280]{1,0:T(8,128)(2,1)S(1)} custom-call(s32[4,16]{1,0:T(4,128)S(1)} %copy-done.2, s32[4,1,2048]{2,1,0:T(1,128)S(1)} %bitcast.23, bf16[128,1280]{1,0:T(8,128)(2,1)S(1)} %bitcast.21, bf16[128,1280]{1,0:T(8,128)(2,1)S(1)} %bitcast.22, bf16[2,320,1280]{2,1,0:T(8,128)(2,1)S(1)} %pad_maximum_fusion.w_ref), custom_call_target="tpu_custom_call" | custom-call | tf_op jit(solution)/shard_map/pallas_call | solution.py:405
  115.5 0.7 copy.9
Async XLA Ops:
  0.8 1.6 %copy-start = (bf16[1,1,128,1280]{3,2,1,0:T(8,128)(2,1)S(1)}, bf16[1,1,128,1280]{3,2,1,0:T(8,128)(2,1)}, u32[]{:S(2)}) copy-start(bf16[1,1,128,1280]{3,2,1,0:T(8,128)(2,1)} %param.7) | copy-start | bytes 983044
  0.8 1.6 %copy-start.1 = (bf16[1,1,128,1280]{3,2,1,0:T(8,128)(2,1)S(1)}, bf16[1,1,128,1280]{3,2,1,0:T(8,128)(2,1)}, u32[]{:S(2)}) copy-start(bf16[1,1,128,1280]{3,2,1,0:T(8,128)(2,1)} %param.8) | copy-start | bytes 983044
  0.8 1.6 %copy-start.2 = (s32[4,16]{1,0:T(4,128)S(1)}, s32[4,16]{1,0:T(4,128)}, u32[]{:S(2)}) copy-start(s32[4,16]{1,0:T(4,128)} %docs_ref.1) | copy-start | bytes 772

commit v2 on v1

--- a/solution.py
+++ b/solution.py
@@ -39,18 +39,19 @@
 
 def kernel(
     docs_ref,
-    doc_row_ref,
     x_ref,
     og_ref,
+    wg_ref,
     w_ref,
     out_ref,
+    acts,
     weights,
-    normed,
     send,
     recv,
     kv_other,
     keys3,
     values,
+    doc_row,
     kv_grad,
     kv_partial,
     back_q,
@@ -59,8 +60,10 @@
     got_kv,
     total,
     branch_out,
+    own_sem,
+    act_send,
+    act_recv,
     w_send,
-    relay_send,
     w_recv,
     send_sem,
     recv_sem,
@@ -80,18 +83,29 @@
     z = lax.axis_index("ctx")
     dp = lax.axis_index("dp")
     x, c = dp // 2, dp % 2
-    z_half, z_low = z // HALF, z % HALF
+    z_half, z_low, page = z // HALF, z % HALF, z % 4
     core_peer = {"dp": 2 * x + 1 - c}
     x_peer = {"dp": 2 * (1 - x) + c}
     before = {"section": (section + n_section - 1) % n_section}
     after = {"section": (section + 1) % n_section}
     alone = z_half == c
+    alone_back = alone & (page == dp)
+    head = 4 * x + 2 * z_half + (z // 4) % 2
 
     def peer(index):
         return {"ctx": HALF * c + index, "dp": 2 * x + z_half}
 
+    def peer_back(index):
+        return {"ctx": HALF * c + index, "dp": page}
+
+    def back_from(index):
+        return {"ctx": HALF * ((index // 2) % 2) + 4 * (index % 2) + dp, "dp": 2 * (index // 4) + z_half}
+
+    own_weights = pltpu.make_async_copy(w_ref, weights.at[dp], own_sem)
+    own_weights.start()
+
     barrier = pltpu.get_barrier_semaphore()
-    for other in (core_peer, x_peer, before, after):
+    for other in (core_peer, x_peer, after):
         pl.semaphore_signal(barrier, inc=1, device_id=other)
 
     def greet(index, carry):
@@ -99,53 +113,47 @@
         def _():
             pl.semaphore_signal(barrier, inc=1, device_id=peer(index))
 
+        @pl.when(jnp.logical_not(alone_back & (index == head)))
+        def _():
+            pl.semaphore_signal(barrier, inc=1, device_id=back_from(index))
+
         return carry
 
     lax.fori_loop(0, HALF, greet, 0)
 
-    def weight_slot(r, j):
-        return 4 * j + 2 * ((x + r // 2) % 2) + (c + r % 2) % 2
-
-    def own_weights(j):
-        return pltpu.make_async_copy(w_ref.at[j], weights.at[weight_slot(0, j)], w_recv.at[0, j])
-
-    def pass_weights(r, j, target, send_sem_ref, arrive_r):
-        block = weights.at[weight_slot(r, j)]
+    def page_of(r):
+        return 2 * ((x + r // 2) % 2) + (c + r % 2) % 2
+
+    def hand_on(buffer, r, target, send_ref, recv_ref):
+        block = buffer.at[page_of(r)]
         return pltpu.make_async_remote_copy(
-            src_ref=block,
-            dst_ref=block,
-            send_sem=send_sem_ref,
-            recv_sem=w_recv.at[arrive_r, j],
-            device_id=target,
-        )
-
-    def to_x(j):
-        return pass_weights(0, j, x_peer, w_send.at[0, j], 2)
-
-    def to_core(j):
-        return pass_weights(0, j, core_peer, w_send.at[1, j], 1)
-
-    def relay(j):
-        return pass_weights(2, j, core_peer, relay_send.at[j], 3)
-
-    def weights_here(r, j):
-        block = weights.at[weight_slot(r, j)]
-        pltpu.make_async_copy(block, block, w_recv.at[r, j]).wait()
-
-    for j in range(2):
-        own_weights(j).start()
+            src_ref=block, dst_ref=block, send_sem=send_ref, recv_sem=recv_ref, device_id=target
+        )
+
+    acts_to_x = hand_on(acts, 0, x_peer, act_send.at[0], act_recv.at[2])
+    acts_to_core = hand_on(acts, 0, core_peer, act_send.at[1], act_recv.at[1])
+    acts_relay = hand_on(acts, 2, core_peer, act_send.at[2], act_recv.at[3])
+    weights_to_x = hand_on(weights, 0, x_peer, w_send.at[0], w_recv.at[2])
+    weights_to_core = hand_on(weights, 0, core_peer, w_send.at[1], w_recv.at[1])
+    weights_relay = hand_on(weights, 2, core_peer, w_send.at[2], w_recv.at[3])
+
+    def here(buffer, r, recv_ref):
+        block = buffer.at[page_of(r)]
+        pltpu.make_async_copy(block, block, recv_ref.at[r]).wait()
 
     inputs = x_ref[...].astype(F32)
     inv_rms = lax.rsqrt(jnp.mean(inputs * inputs, axis=-1, keepdims=True) + 1e-05)
-    normed[...] = (inputs * inv_rms).astype(BF16)
-
-    own_weights(0).wait()
-    own_weights(1).wait()
-    pl.semaphore_wait(barrier, 12 - alone.astype(jnp.int32))
-    for j in range(2):
-        to_x(j).start()
-    for j in range(2):
-        to_core(j).start()
+    acts[dp, 0:BLOCK] = (inputs * inv_rms).astype(BF16)
+    acts[dp, BLOCK : 2 * BLOCK] = og_ref[...]
+    for block in range(N_CTX):
+        doc_row[:, block * BLOCK : (block + 1) * BLOCK] = jnp.full(
+            (1, BLOCK), docs_ref[page, block], jnp.int32
+        )
+
+    pl.semaphore_wait(barrier, 19 - alone.astype(jnp.int32) - alone_back.astype(jnp.int32))
+    acts_to_x.start()
+    acts_to_core.start()
+    own_weights.wait()
 
     def send_copy(index):
         return pltpu.make_async_remote_copy(
@@ -156,20 +164,20 @@
             device_id=peer(index),
         )
 
-    def project(slot):
-        w = weights.at[slot]
-        qkv = dot_nt(w[0:H3], normed[...])
-        out_grad = dot_nt(w[H3:H4], og_ref[...])
+    def project(slot, j):
+        qkv = dot_nt(weights[dp, j], acts[slot, 0:BLOCK])
+        out_grad = dot_nt(wg_ref[j], acts[slot, BLOCK : 2 * BLOCK])
         q_high, q_low = split(qkv[0:H1])
         k_high, k_low = split(qkv[H1:H2])
-        message = send.at[slot]
+        unit = 4 * j + slot
+        message = send.at[unit]
         message[0:H1] = q_high
         message[H1:H2] = q_low
         message[H2:H3] = out_grad.astype(BF16)
         message[H3:H4] = k_high
         message[H4 : H4 + H1] = k_low
         message[H4 + H1 : H6] = qkv[H2:H3].astype(BF16)
-        mine = alone & (slot == z_low)
+        mine = alone & (unit == z_low)
 
         @pl.when(mine)
         def _():
@@ -177,32 +185,24 @@
 
         @pl.when(jnp.logical_not(mine))
         def _():
-            send_copy(slot).start()
-
-    def near(t, carry):
-        r, j = t // 2, t % 2
-
-        @pl.when(r == 1)
-        def _():
-            weights_here(1, j)
-
-        project(weight_slot(r, j))
-        return carry
-
-    lax.fori_loop(0, 4, near, 0)
-
-    def far(t, carry):
-        r, j = 2 + t % 2, t // 2
-        weights_here(r, j)
+            send_copy(unit).start()
+
+    def step(r, carry):
+        @pl.when(r > 0)
+        def _():
+            here(acts, r, act_recv)
 
         @pl.when(r == 2)
         def _():
-            relay(j).start()
-
-        project(weight_slot(r, j))
-        return carry
-
-    lax.fori_loop(0, 4, far, 0)
+            acts_relay.start()
+            weights_to_x.start()
+            weights_to_core.start()
+
+        project(page_of(r), 0)
+        project(page_of(r), 1)
+        return carry
+
+    lax.fori_loop(0, 4, step, 0)
 
     def kv_copy(index):
         return pltpu.make_async_remote_copy(
@@ -235,30 +235,25 @@
 
     lax.fori_loop(0, HALF, arrive_other, 0)
 
-    page = 2 * x + z_half
-    doc_row = doc_row_ref[page]
     kv_grad[...] = jnp.zeros_like(kv_grad)
 
     def return_q(index):
         return pltpu.make_async_remote_copy(
             src_ref=back_q.at[index],
-            dst_ref=got_q.at[z_low],
+            dst_ref=got_q.at[head],
             send_sem=bq_send.at[index],
-            recv_sem=bq_recv.at[z_low],
+            recv_sem=bq_recv.at[head],
             device_id=peer_back(index),
         )
 
     def return_kv(index):
         return pltpu.make_async_remote_copy(
             src_ref=back_kv.at[index],
-            dst_ref=got_kv.at[z_low],
+            dst_ref=got_kv.at[head],
             send_sem=bkv_send.at[index],
-            recv_sem=bkv_recv.at[z_low],
+            recv_sem=bkv_recv.at[head],
             device_id=peer_back(index),
         )
-
-    def peer_back(index):
-        return peer(index)
 
     def attend(chunk, carry):
         one, two = recv.at[2 * chunk], recv.at[2 * chunk + 1]
@@ -269,7 +264,7 @@
         first = docs_ref[page, HALF * c + 2 * chunk]
         second = docs_ref[page, HALF * c + 2 * chunk + 1]
         rows = lax.broadcasted_iota(jnp.int32, (2 * BLOCK, 1), 0)
-        allowed = jnp.where(rows < BLOCK, first, second) == doc_row
+        allowed = jnp.where(rows < BLOCK, first, second) == doc_row[...]
         scores = jnp.where(allowed, dot(q3, keys3[...]) * SCALE, NEG)
         top = jnp.max(scores, axis=-1, keepdims=True)
         weight = jnp.exp(scores - top)
@@ -287,12 +282,12 @@
         kv_grad[H1:H2] += dot(g_flat, prob.astype(BF16))
         for side in range(2):
             index = 2 * chunk + side
-            mine = alone & (index == z_low)
+            mine = alone_back & (index == z_low)
 
             @pl.when(mine)
             def _():
                 pltpu.make_async_copy(
-                    back_q.at[index], got_q.at[z_low], bq_recv.at[z_low]
+                    back_q.at[index], got_q.at[head], bq_recv.at[head]
                 ).start()
 
             @pl.when(jnp.logical_not(mine))
@@ -320,12 +315,12 @@
         mine_lanes = pl.ds(pl.multiple_of((HALF * c + index) * BLOCK, BLOCK), BLOCK)
         lanes = pl.ds(pl.multiple_of(index * BLOCK, BLOCK), BLOCK)
         back_kv[index] = (kv_grad[:, mine_lanes] + kv_partial[:, lanes]).astype(BF16)
-        mine = alone & (index == z_low)
+        mine = alone_back & (index == z_low)
 
         @pl.when(mine)
         def _():
             pltpu.make_async_copy(
-                back_kv.at[index], got_kv.at[z_low], bkv_recv.at[z_low]
+                back_kv.at[index], got_kv.at[head], bkv_recv.at[head]
             ).start()
 
         @pl.when(jnp.logical_not(mine))
@@ -336,14 +331,18 @@
 
     lax.fori_loop(0, HALF, finish_kv, 0)
 
+    here(weights, 1, w_recv)
+    here(weights, 2, w_recv)
+    weights_relay.start()
     total[...] = jnp.zeros_like(total)
+    here(weights, 3, w_recv)
 
     def combine(index, carry):
         q_block, kv_block = got_q.at[index], got_kv.at[index]
         pltpu.make_async_copy(q_block, q_block, bq_recv.at[index]).wait()
         pltpu.make_async_copy(kv_block, kv_block, bkv_recv.at[index]).wait()
         grads = jnp.concatenate([q_block[...], kv_block[...]], axis=0)
-        total[...] += dot(flip(grads), weights[index, 0:H3])
+        total[...] += dot(flip(grads), weights[index // 2, index % 2])
         return carry
 
     lax.fori_loop(0, HALF, combine, 0)
@@ -363,10 +362,10 @@
     )
     shift.start()
 
-    for j in range(2):
-        to_x(j).wait_send()
-        to_core(j).wait_send()
-        relay(j).wait_send()
+    for sent in (acts_to_x, acts_to_core, acts_relay):
+        sent.wait_send()
+    for sent in (weights_to_x, weights_to_core, weights_relay):
+        sent.wait_send()
     partial.wait_send()
 
     def drain(index, carry):
@@ -375,6 +374,9 @@
         @pl.when(jnp.logical_not(alone & (index == z_low)))
         def _():
             send_copy(index).wait_send()
+
+        @pl.when(jnp.logical_not(alone_back & (index == z_low)))
+        def _():
             return_q(index).wait_send()
             return_kv(index).wait_send()
 
@@ -391,15 +393,9 @@
         return weight[0].T.reshape(2, HEAD_DIM, WIDTH)
 
     weights = jnp.concatenate(
-        [
-            by_head(query_weight),
-            by_head(key_weight),
-            by_head(value_weight),
-            out_weight[0].reshape(2, HEAD_DIM, WIDTH),
-        ],
-        axis=1,
+        [by_head(query_weight), by_head(key_weight), by_head(value_weight)], axis=1
     )
-    doc_row = jnp.repeat(doc_ids, BLOCK, axis=1)[:, None, :]
+    out_heads = out_weight[0].reshape(2, HEAD_DIM, WIDTH)
     vmem = pl.BlockSpec(memory_space=pltpu.VMEM)
     dma = pltpu.SemaphoreType.DMA
     out = pl.pallas_call(
@@ -414,13 +410,14 @@
         ],
         out_specs=vmem,
         scratch_shapes=[
-            pltpu.VMEM((HALF, H4, WIDTH), BF16),
-            pltpu.VMEM((BLOCK, WIDTH), BF16),
+            pltpu.VMEM((4, 2 * BLOCK, WIDTH), BF16),
+            pltpu.VMEM((4, 2, H3, WIDTH), BF16),
             pltpu.VMEM((HALF, H6, BLOCK), BF16),
             pltpu.VMEM((HALF, H6, BLOCK), BF16),
             pltpu.VMEM((HALF, H3, BLOCK), BF16),
             pltpu.VMEM((H3, N_CTX * BLOCK), BF16),
             pltpu.VMEM((H1, N_CTX * BLOCK), BF16),
+            pltpu.VMEM((1, N_CTX * BLOCK), jnp.int32),
             pltpu.VMEM((H2, N_CTX * BLOCK), F32),
             pltpu.VMEM((H2, HALF * BLOCK), F32),
             pltpu.VMEM((HALF, H1, BLOCK), BF16),
@@ -429,9 +426,11 @@
             pltpu.VMEM((HALF, H2, BLOCK), BF16),
             pltpu.VMEM((BLOCK, WIDTH), F32),
             pltpu.VMEM((BLOCK, WIDTH), BF16),
-            dma((2, 2)),
-            dma((2,)),
-            dma((4, 2)),
+            dma,
+            dma((3,)),
+            dma((4,)),
+            dma((3,)),
+            dma((4,)),
             dma((HALF,)),
             dma((HALF,)),
             dma((HALF,)),
@@ -448,7 +447,7 @@
         compiler_params=pltpu.CompilerParams(
             collective_id=0, has_side_effects=True, vmem_limit_bytes=48 * 2**20
         ),
-    )(doc_ids, doc_row, activations[0, 0], out_grads[0, 0], weights)
+    )(doc_ids, activations[0, 0], out_grads[0, 0], out_heads, weights)
     return out[None, None]
 
 

time: 116 us -> 107 us (0.922)
  the two profiles are of different devices: /device:TPU:159 before, /device:TPU:70 now
where the time goes in v2:
time: 107 us
  Pallas kernels  105 us (98%)
  other arithmetic  1.42 us (1%)
    pallas_call x1, Pallas kernels, body(): pl.pallas_call(kernel, out_shape=jax.ShapeDtypeStruct((tokens, WIDTH), BF...  105 us

profile of v2, /device:TPU:70, one launch (start us, length us, event | category | flops | bytes accessed | tf_op | source)
XLA Modules:
  0.0 107.1 jit_solution(14058091199004591598)
XLA Ops:
  0.0 0.0 copy-start
  0.0 0.0 copy-start.1
  0.0 0.0 copy-start.2
  0.0 0.0 copy-start.3
  0.0 1.4 %pad_maximum_fusion.w_ref = bf16[2,240,1280]{2,1,0:T(8,128)(2,1)S(1)} fusion(bf16[2,80,1280]{2,1,0:T(8,128)(2,1)} %bitcast.23, bf16[2,80,1280]{2,1,0:T(8,128)(2,1)} %bitcast.24, bf16[2,80,1280]{2,1,0:T(8,128)(2,1)} %bitcast.25), kind=kLoop, calls=%fused_computation | loop fusion | flops 3686400 | bytes 2457600 | tf_op jit(solution)/shard_map/concatenate | solution.py:395
  1.4 0.0 copy-done
  1.5 0.0 copy-done.1
  1.5 0.1 copy-done.2
  1.6 0.0 copy-done.3
  1.6 104.8 %shard_map.73 = bf16[128,1280]{1,0:T(8,128)(2,1)S(1)} custom-call(s32[4,16]{1,0:T(4,128)S(1)} %copy-done.3, bf16[128,1280]{1,0:T(8,128)(2,1)S(1)} %bitcast.21, bf16[128,1280]{1,0:T(8,128)(2,1)S(1)} %bitcast.22, bf16[2,80,1280]{2,1,0:T(8,128)(2,1)S(1)} %bitcast.20, bf16[2,240,1280]{2,1,0:T(8,128)(2,1)S(1)} %pad_maximum_fusion.w_ref), custom_call_target="tpu_custom_call" | custom-call | tf_op jit(solution)/shard_map/pallas_call | solution.py:401
  106.4 0.7 copy.9
Async XLA Ops:
  0.0 1.4 %copy-start = (bf16[1,160,1280]{2,1,0:T(8,128)(2,1)S(1)}, bf16[1,160,1280]{2,1,0:T(8,128)(2,1)}, u32[]{:S(2)}) copy-start(bf16[1,160,1280]{2,1,0:T(8,128)(2,1)} %param.13) | copy-start | bytes 1228804
  0.0 1.5 %copy-start.1 = (bf16[1,1,128,1280]{3,2,1,0:T(8,128)(2,1)S(1)}, bf16[1,1,128,1280]{3,2,1,0:T(8,128)(2,1)}, u32[]{:S(2)}) copy-start(bf16[1,1,128,1280]{3,2,1,0:T(8,128)(2,1)} %param.7) | copy-start | bytes 983044
  0.0 1.6 %copy-start.2 = (bf16[1,1,128,1280]{3,2,1,0:T(8,128)(2,1)S(1)}, bf16[1,1,128,1280]{3,2,1,0:T(8,128)(2,1)}, u32[]{:S(2)}) copy-start(bf16[1,1,128,1280]{3,2,1,0:T(8,128)(2,1)} %param.8) | copy-start | bytes 983044
  0.0 1.6 %copy-start.3 = (s32[4,16]{1,0:T(4,128)S(1)}, s32[4,16]{1,0:T(4,128)}, u32[]{:S(2)}) copy-start(s32[4,16]{1,0:T(4,128)} %docs_ref.1) | copy-start | bytes 772

commit v3 on v2

--- a/solution.py
+++ b/solution.py
@@ -39,11 +39,15 @@
 
 def kernel(
     docs_ref,
+    x_hbm,
+    og_hbm,
+    wq_hbm,
+    wk_hbm,
+    wv_hbm,
+    wg_hbm,
+    out_ref,
     x_ref,
-    og_ref,
     wg_ref,
-    w_ref,
-    out_ref,
     acts,
     weights,
     send,
@@ -51,7 +55,6 @@
     kv_other,
     keys3,
     values,
-    doc_row,
     kv_grad,
     kv_partial,
     back_q,
@@ -60,7 +63,7 @@
     got_kv,
     total,
     branch_out,
-    own_sem,
+    load_sem,
     act_send,
     act_recv,
     w_send,
@@ -90,6 +93,7 @@
     after = {"section": (section + 1) % n_section}
     alone = z_half == c
     alone_back = alone & (page == dp)
+    late = page // 2 != x
     head = 4 * x + 2 * z_half + (z // 4) % 2
 
     def peer(index):
@@ -100,9 +104,6 @@
 
     def back_from(index):
         return {"ctx": HALF * ((index // 2) % 2) + 4 * (index % 2) + dp, "dp": 2 * (index // 4) + z_half}
-
-    own_weights = pltpu.make_async_copy(w_ref, weights.at[dp], own_sem)
-    own_weights.start()
 
     barrier = pltpu.get_barrier_semaphore()
     for other in (core_peer, x_peer, after):
@@ -120,6 +121,28 @@
         return carry
 
     lax.fori_loop(0, HALF, greet, 0)
+
+    loads = [
+        pltpu.make_async_copy(source, target, load_sem.at[number])
+        for number, (source, target) in enumerate(
+            (
+                (x_hbm, x_ref),
+                (wq_hbm, weights.at[dp, :, pl.ds(0, H1)]),
+                (wk_hbm, weights.at[dp, :, pl.ds(H1, H1)]),
+                (wv_hbm, weights.at[dp, :, pl.ds(H2, H1)]),
+                (og_hbm, acts.at[dp, pl.ds(BLOCK, BLOCK)]),
+                (wg_hbm, wg_ref),
+            )
+        )
+    ]
+    for load in loads:
+        load.start()
+
+    rows = lax.broadcasted_iota(jnp.int32, (16, BLOCK), 0)
+    for block in range(N_CTX):
+        keys3[H3 : H3 + 16, block * BLOCK : (block + 1) * BLOCK] = jnp.where(
+            (rows == docs_ref[page, block]) | (rows >= 4), 0.0, NEG
+        ).astype(BF16)
 
     def page_of(r):
         return 2 * ((x + r // 2) % 2) + (c + r % 2) % 2
@@ -141,19 +164,12 @@
         block = buffer.at[page_of(r)]
         pltpu.make_async_copy(block, block, recv_ref.at[r]).wait()
 
+    loads[0].wait()
     inputs = x_ref[...].astype(F32)
     inv_rms = lax.rsqrt(jnp.mean(inputs * inputs, axis=-1, keepdims=True) + 1e-05)
     acts[dp, 0:BLOCK] = (inputs * inv_rms).astype(BF16)
-    acts[dp, BLOCK : 2 * BLOCK] = og_ref[...]
-    for block in range(N_CTX):
-        doc_row[:, block * BLOCK : (block + 1) * BLOCK] = jnp.full(
-            (1, BLOCK), docs_ref[page, block], jnp.int32
-        )
-
-    pl.semaphore_wait(barrier, 19 - alone.astype(jnp.int32) - alone_back.astype(jnp.int32))
-    acts_to_x.start()
-    acts_to_core.start()
-    own_weights.wait()
+    for load in loads[1:]:
+        load.wait()
 
     def send_copy(index):
         return pltpu.make_async_remote_copy(
@@ -167,7 +183,7 @@
     def project(slot, j):
         qkv = dot_nt(weights[dp, j], acts[slot, 0:BLOCK])
         out_grad = dot_nt(wg_ref[j], acts[slot, BLOCK : 2 * BLOCK])
-        q_high, q_low = split(qkv[0:H1])
+        q_high, q_low = split(qkv[0:H1] * SCALE)
         k_high, k_low = split(qkv[H1:H2])
         unit = 4 * j + slot
         message = send.at[unit]
@@ -177,6 +193,9 @@
         message[H3:H4] = k_high
         message[H4 : H4 + H1] = k_low
         message[H4 + H1 : H6] = qkv[H2:H3].astype(BF16)
+
+    def dispatch(unit):
+        message = send.at[unit]
         mine = alone & (unit == z_low)
 
         @pl.when(mine)
@@ -187,10 +206,16 @@
         def _():
             send_copy(unit).start()
 
+    project(dp, 0)
+    project(dp, 1)
+    pl.semaphore_wait(barrier, 19 - alone.astype(jnp.int32) - alone_back.astype(jnp.int32))
+    acts_to_x.start()
+    acts_to_core.start()
+    dispatch(dp)
+    dispatch(4 + dp)
+
     def step(r, carry):
-        @pl.when(r > 0)
-        def _():
-            here(acts, r, act_recv)
+        here(acts, r, act_recv)
 
         @pl.when(r == 2)
         def _():
@@ -198,11 +223,12 @@
             weights_to_x.start()
             weights_to_core.start()
 
-        project(page_of(r), 0)
-        project(page_of(r), 1)
-        return carry
-
-    lax.fori_loop(0, 4, step, 0)
+        for j in range(2):
+            project(page_of(r), j)
+            dispatch(4 * j + page_of(r))
+        return carry
+
+    lax.fori_loop(1, 4, step, 0)
 
     def kv_copy(index):
         return pltpu.make_async_remote_copy(
@@ -255,17 +281,34 @@
             device_id=peer_back(index),
         )
 
-    def attend(chunk, carry):
+    def give_q(index):
+        mine = alone_back & (index == z_low)
+
+        @pl.when(mine)
+        def _():
+            pltpu.make_async_copy(back_q.at[index], got_q.at[head], bq_recv.at[head]).start()
+
+        @pl.when(jnp.logical_not(mine))
+        def _():
+            return_q(index).start()
+
+    def in_order(step, count):
+        return c * (count - 1) + (1 - 2 * c) * step
+
+    def attend(step, carry):
+        chunk = in_order(step, HALF // 2)
         one, two = recv.at[2 * chunk], recv.at[2 * chunk + 1]
         q_pair = jnp.concatenate([one[0:H2], two[0:H2]], axis=1)
         g_flat = jnp.concatenate([one[H2:H3], two[H2:H3]], axis=1)
-        q3 = flip(jnp.concatenate([q_pair[0:H1], q_pair], axis=0))
         g = flip(g_flat)
         first = docs_ref[page, HALF * c + 2 * chunk]
         second = docs_ref[page, HALF * c + 2 * chunk + 1]
-        rows = lax.broadcasted_iota(jnp.int32, (2 * BLOCK, 1), 0)
-        allowed = jnp.where(rows < BLOCK, first, second) == doc_row[...]
-        scores = jnp.where(allowed, dot(q3, keys3[...]) * SCALE, NEG)
+        shape = (16, 2 * BLOCK)
+        lanes = lax.broadcasted_iota(jnp.int32, shape, 1)
+        document = jnp.where(lanes < BLOCK, first, second)
+        which = (lax.broadcasted_iota(jnp.int32, shape, 0) == document).astype(F32).astype(BF16)
+        q3 = flip(jnp.concatenate([q_pair[0:H1], q_pair, which], axis=0))
+        scores = dot(q3, keys3[...])
         top = jnp.max(scores, axis=-1, keepdims=True)
         weight = jnp.exp(scores - top)
         share = 1.0 / jnp.sum(weight, axis=-1, keepdims=True)
@@ -278,21 +321,12 @@
         back_q[2 * chunk] = q_grad[:, 0:BLOCK]
         back_q[2 * chunk + 1] = q_grad[:, BLOCK:]
         k_grad = dot(q_pair, dscore)
-        kv_grad[0:H1] += (k_grad[0:H1] + k_grad[H1:H2]) * SCALE
+        kv_grad[0:H1] += k_grad[0:H1] + k_grad[H1:H2]
         kv_grad[H1:H2] += dot(g_flat, prob.astype(BF16))
-        for side in range(2):
-            index = 2 * chunk + side
-            mine = alone_back & (index == z_low)
-
-            @pl.when(mine)
-            def _():
-                pltpu.make_async_copy(
-                    back_q.at[index], got_q.at[head], bq_recv.at[head]
-                ).start()
-
-            @pl.when(jnp.logical_not(mine))
-            def _():
-                return_q(index).start()
+        @pl.when(late)
+        def _():
+            give_q(2 * chunk + c)
+            give_q(2 * chunk + 1 - c)
 
         return carry
 
@@ -311,7 +345,22 @@
     partial.start()
     partial.wait_recv()
 
-    def finish_kv(index, carry):
+    def sent_all(index, carry):
+        @pl.when(jnp.logical_not(alone & (index == z_low)))
+        def _():
+            send_copy(index).wait_send()
+
+        return carry
+
+    lax.fori_loop(0, HALF, sent_all, 0)
+
+    def finish_kv(step, carry):
+        index = in_order(step, HALF)
+
+        @pl.when(jnp.logical_not(late))
+        def _():
+            give_q(index)
+
         mine_lanes = pl.ds(pl.multiple_of((HALF * c + index) * BLOCK, BLOCK), BLOCK)
         lanes = pl.ds(pl.multiple_of(index * BLOCK, BLOCK), BLOCK)
         back_kv[index] = (kv_grad[:, mine_lanes] + kv_partial[:, lanes]).astype(BF16)
@@ -337,7 +386,8 @@
     total[...] = jnp.zeros_like(total)
     here(weights, 3, w_recv)
 
-    def combine(index, carry):
+    def combine(step, carry):
+        index = (4 * x + step) % HALF
         q_block, kv_block = got_q.at[index], got_kv.at[index]
         pltpu.make_async_copy(q_block, q_block, bq_recv.at[index]).wait()
         pltpu.make_async_copy(kv_block, kv_block, bkv_recv.at[index]).wait()
@@ -371,10 +421,6 @@
     def drain(index, carry):
         kv_copy(index).wait_send()
 
-        @pl.when(jnp.logical_not(alone & (index == z_low)))
-        def _():
-            send_copy(index).wait_send()
-
         @pl.when(jnp.logical_not(alone_back & (index == z_low)))
         def _():
             return_q(index).wait_send()
@@ -389,35 +435,30 @@
 def body(activations, out_grads, doc_ids, query_weight, key_weight, value_weight, out_weight):
     tokens = activations.shape[2]
 
-    def by_head(weight):
-        return weight[0].T.reshape(2, HEAD_DIM, WIDTH)
-
-    weights = jnp.concatenate(
-        [by_head(query_weight), by_head(key_weight), by_head(value_weight)], axis=1
-    )
-    out_heads = out_weight[0].reshape(2, HEAD_DIM, WIDTH)
+    def stay(array):
+        return pltpu.with_memory_space_constraint(array, pltpu.HBM)
+
+    def by_head(rows):
+        return stay(rows.reshape(2, HEAD_DIM, WIDTH))
+
+    anywhere = pl.BlockSpec(memory_space=pl.ANY)
     vmem = pl.BlockSpec(memory_space=pltpu.VMEM)
     dma = pltpu.SemaphoreType.DMA
     out = pl.pallas_call(
         kernel,
         out_shape=jax.ShapeDtypeStruct((tokens, WIDTH), BF16),
-        in_specs=[
-            pl.BlockSpec(memory_space=pltpu.SMEM),
-            vmem,
-            vmem,
-            vmem,
-            pl.BlockSpec(memory_space=pl.ANY),
-        ],
+        in_specs=[pl.BlockSpec(memory_space=pltpu.SMEM)] + [anywhere] * 6,
         out_specs=vmem,
         scratch_shapes=[
+            pltpu.VMEM((BLOCK, WIDTH), BF16),
+            pltpu.VMEM((2, HEAD_DIM, WIDTH), BF16),
             pltpu.VMEM((4, 2 * BLOCK, WIDTH), BF16),
             pltpu.VMEM((4, 2, H3, WIDTH), BF16),
             pltpu.VMEM((HALF, H6, BLOCK), BF16),
             pltpu.VMEM((HALF, H6, BLOCK), BF16),
             pltpu.VMEM((HALF, H3, BLOCK), BF16),
-            pltpu.VMEM((H3, N_CTX * BLOCK), BF16),
+            pltpu.VMEM((H3 + 16, N_CTX * BLOCK), BF16),
             pltpu.VMEM((H1, N_CTX * BLOCK), BF16),
-            pltpu.VMEM((1, N_CTX * BLOCK), jnp.int32),
             pltpu.VMEM((H2, N_CTX * BLOCK), F32),
             pltpu.VMEM((H2, HALF * BLOCK), F32),
             pltpu.VMEM((HALF, H1, BLOCK), BF16),
@@ -426,7 +467,7 @@
             pltpu.VMEM((HALF, H2, BLOCK), BF16),
             pltpu.VMEM((BLOCK, WIDTH), F32),
             pltpu.VMEM((BLOCK, WIDTH), BF16),
-            dma,
+            dma((6,)),
             dma((3,)),
             dma((4,)),
             dma((3,)),
@@ -447,7 +488,15 @@
         compiler_params=pltpu.CompilerParams(
             collective_id=0, has_side_effects=True, vmem_limit_bytes=48 * 2**20
         ),
-    )(doc_ids, activations[0, 0], out_grads[0, 0], out_heads, weights)
+    )(
+        doc_ids,
+        stay(activations[0, 0]),
+        stay(out_grads[0, 0]),
+        by_head(query_weight[0].T),
+        by_head(key_weight[0].T),
+        by_head(value_weight[0].T),
+        by_head(out_weight[0]),
+    )
     return out[None, None]
 
 

time: 107 us -> 102 us (0.953)
  the two profiles are of different devices: /device:TPU:70 before, /device:TPU:203 now
where the time goes in v3:
time: 102 us
  Pallas kernels  101 us (99%)
  local copies, waits for them, and re-layouts  1.41 us (1%)
    pallas_call x1, Pallas kernels, body(): pl.pallas_call(kernel, out_shape=jax.ShapeDtypeStruct((tokens, WIDTH), BF...  101 us

profile of v3, /device:TPU:203, one launch (start us, length us, event | category | flops | bytes accessed | tf_op | source)
XLA Modules:
  0.0 102.2 jit_solution(7002713167151819555)
XLA Ops:
  0.0 0.0 copy-start
  0.0 0.7 copy-done
  0.7 100.8 %shard_map.73 = bf16[128,1280]{1,0:T(8,128)(2,1)S(1)} custom-call(s32[4,16]{1,0:T(4,128)S(1)} %copy-done, bf16[128,1280]{1,0:T(8,128)(2,1)} %bitcast.24, bf16[128,1280]{1,0:T(8,128)(2,1)} %bitcast.25, bf16[2,80,1280]{2,1,0:T(8,128)(2,1)} %bitcast.20, bf16[2,80,1280]{2,1,0:T(8,128)(2,1)} %bitcast.21, bf16[2,80,1280]{2,1,0:T(8,128)(2,1)} %bitcast.22, ...), custom_call_target="tpu_custom_call" | custom-call | tf_op jit(solution)/shard_map/pallas_call | solution.py:447
  101.5 0.7 copy.9
Async XLA Ops:
  0.0 0.7 copy-start

commit v4 on v3

--- a/solution.py
+++ b/solution.py
@@ -26,6 +26,10 @@
 
 def dot_nt(a, b):
     return lax.dot_general(a, b, NT, preferred_element_type=F32)
+
+
+def swap(two_bits):
+    return 2 * (two_bits % 2) + two_bits // 2
 
 
 def flip(matrix):
@@ -86,7 +90,7 @@
     z = lax.axis_index("ctx")
     dp = lax.axis_index("dp")
     x, c = dp // 2, dp % 2
-    z_half, z_low, page = z // HALF, z % HALF, z % 4
+    z_half, z_low, page = z // HALF, z % HALF, swap(z % 4)
     core_peer = {"dp": 2 * x + 1 - c}
     x_peer = {"dp": 2 * (1 - x) + c}
     before = {"section": (section + n_section - 1) % n_section}
@@ -103,7 +107,7 @@
         return {"ctx": HALF * c + index, "dp": page}
 
     def back_from(index):
-        return {"ctx": HALF * ((index // 2) % 2) + 4 * (index % 2) + dp, "dp": 2 * (index // 4) + z_half}
+        return {"ctx": HALF * ((index // 2) % 2) + 4 * (index % 2) + swap(dp), "dp": 2 * (index // 4) + z_half}
 
     barrier = pltpu.get_barrier_semaphore()
     for other in (core_peer, x_peer, after):
@@ -185,7 +189,7 @@
         out_grad = dot_nt(wg_ref[j], acts[slot, BLOCK : 2 * BLOCK])
         q_high, q_low = split(qkv[0:H1] * SCALE)
         k_high, k_low = split(qkv[H1:H2])
-        unit = 4 * j + slot
+        unit = 4 * j + swap(slot)
         message = send.at[unit]
         message[0:H1] = q_high
         message[H1:H2] = q_low
@@ -211,8 +215,8 @@
     pl.semaphore_wait(barrier, 19 - alone.astype(jnp.int32) - alone_back.astype(jnp.int32))
     acts_to_x.start()
     acts_to_core.start()
-    dispatch(dp)
-    dispatch(4 + dp)
+    dispatch(swap(dp))
+    dispatch(4 + swap(dp))
 
     def step(r, carry):
         here(acts, r, act_recv)
@@ -225,7 +229,7 @@
 
         for j in range(2):
             project(page_of(r), j)
-            dispatch(4 * j + page_of(r))
+            dispatch(4 * j + swap(page_of(r)))
         return carry
 
     lax.fori_loop(1, 4, step, 0)
@@ -323,8 +327,7 @@
         k_grad = dot(q_pair, dscore)
         kv_grad[0:H1] += k_grad[0:H1] + k_grad[H1:H2]
         kv_grad[H1:H2] += dot(g_flat, prob.astype(BF16))
-        @pl.when(late)
-        def _():
+        if True:
             give_q(2 * chunk + c)
             give_q(2 * chunk + 1 - c)
 
@@ -356,10 +359,6 @@
 
     def finish_kv(step, carry):
         index = in_order(step, HALF)
-
-        @pl.when(jnp.logical_not(late))
-        def _():
-            give_q(index)
 
         mine_lanes = pl.ds(pl.multiple_of((HALF * c + index) * BLOCK, BLOCK), BLOCK)
         lanes = pl.ds(pl.multiple_of(index * BLOCK, BLOCK), BLOCK)

time: 102 us -> 101 us (level)
  the two profiles are of different devices: /device:TPU:203 before, /device:TPU:33 now
where the time goes in v4:
time: 101 us; the launch traced here: 100 us
  Pallas kernels  98.9 us (98%)
  local copies, waits for them, and re-layouts  1.41 us (1%)
    pallas_call x1, Pallas kernels, body(): pl.pallas_call(kernel, out_shape=jax.ShapeDtypeStruct((tokens, WIDTH), BF...  98.9 us

profile of v4, /device:TPU:33, one launch (start us, length us, event | category | flops | bytes accessed | tf_op | source)
XLA Modules:
  0.0 100.3 jit_solution(10736538432091047293)
XLA Ops:
  0.0 0.0 copy-start
  0.0 0.7 copy-done
  0.7 98.9 %shard_map.73 = bf16[128,1280]{1,0:T(8,128)(2,1)S(1)} custom-call(s32[4,16]{1,0:T(4,128)S(1)} %copy-done, bf16[128,1280]{1,0:T(8,128)(2,1)} %bitcast.24, bf16[128,1280]{1,0:T(8,128)(2,1)} %bitcast.25, bf16[2,80,1280]{2,1,0:T(8,128)(2,1)} %bitcast.20, bf16[2,80,1280]{2,1,0:T(8,128)(2,1)} %bitcast.21, bf16[2,80,1280]{2,1,0:T(8,128)(2,1)} %bitcast.22, ...), custom_call_target="tpu_custom_call" | custom-call | tf_op jit(solution)/shard_map/pallas_call | solution.py:446
  99.6 0.7 copy.9
Async XLA Ops:
  0.0 0.7 copy-start

commit v5 on v4

--- a/solution.py
+++ b/solution.py
@@ -215,24 +215,34 @@
     pl.semaphore_wait(barrier, 19 - alone.astype(jnp.int32) - alone_back.astype(jnp.int32))
     acts_to_x.start()
     acts_to_core.start()
-    dispatch(swap(dp))
-    dispatch(4 + swap(dp))
-
-    def step(r, carry):
-        here(acts, r, act_recv)
-
-        @pl.when(r == 2)
-        def _():
+    def step(turn, carry):
+        r = 2 * (turn // 2) + (turn + c * (turn // 2)) % 2
+
+        @pl.when(r == 1)
+        def _():
+            here(acts, 1, act_recv)
+
+        @pl.when(turn == 2)
+        def _():
+            here(acts, 2, act_recv)
             acts_relay.start()
             weights_to_x.start()
             weights_to_core.start()
 
-        for j in range(2):
-            project(page_of(r), j)
-            dispatch(4 * j + swap(page_of(r)))
-        return carry
-
-    lax.fori_loop(1, 4, step, 0)
+        @pl.when(r == 3)
+        def _():
+            here(acts, 3, act_recv)
+
+        @pl.when(r > 0)
+        def _():
+            project(page_of(r), 0)
+            project(page_of(r), 1)
+
+        dispatch(swap(page_of(r)))
+        dispatch(4 + swap(page_of(r)))
+        return carry
+
+    lax.fori_loop(0, 4, step, 0)
 
     def kv_copy(index):
         return pltpu.make_async_remote_copy(
@@ -355,7 +365,6 @@
 
         return carry
 
-    lax.fori_loop(0, HALF, sent_all, 0)
 
     def finish_kv(step, carry):
         index = in_order(step, HALF)
@@ -428,6 +437,7 @@
         return carry
 
     lax.fori_loop(0, HALF, drain, 0)
+    lax.fori_loop(0, HALF, sent_all, 0)
     shift.wait()
 
 

time: 101 us -> 98.1 us (0.971)
  the two profiles are of different devices: /device:TPU:33 before, /device:TPU:157 now
where the time goes in v5:
time: 98.1 us; the launch traced here: 97.9 us
  Pallas kernels  96.5 us (98%)
  local copies, waits for them, and re-layouts  1.41 us (1%)
    pallas_call x1, Pallas kernels, body(): pl.pallas_call(kernel, out_shape=jax.ShapeDtypeStruct((tokens, WIDTH), BF...  96.5 us

profile of v5, /device:TPU:157, one launch (start us, length us, event | category | flops | bytes accessed | tf_op | source)
XLA Modules:
  0.0 97.9 jit_solution(11538482045106981209)
XLA Ops:
  0.0 0.0 copy-start
  0.0 0.7 copy-done
  0.7 96.5 %shard_map.73 = bf16[128,1280]{1,0:T(8,128)(2,1)S(1)} custom-call(s32[4,16]{1,0:T(4,128)S(1)} %copy-done, bf16[128,1280]{1,0:T(8,128)(2,1)} %bitcast.24, bf16[128,1280]{1,0:T(8,128)(2,1)} %bitcast.25, bf16[2,80,1280]{2,1,0:T(8,128)(2,1)} %bitcast.20, bf16[2,80,1280]{2,1,0:T(8,128)(2,1)} %bitcast.21, bf16[2,80,1280]{2,1,0:T(8,128)(2,1)} %bitcast.22, ...), custom_call_target="tpu_custom_call" | custom-call | tf_op jit(solution)/shard_map/pallas_call | solution.py:456
  97.2 0.7 copy.9
Async XLA Ops:
  0.0 0.7 copy-start

commit v6 on v5

--- a/solution.py
+++ b/solution.py
@@ -66,6 +66,8 @@
     got_q,
     got_kv,
     total,
+    rms_kept,
+    cubed,
     branch_out,
     load_sem,
     act_send,
@@ -233,13 +235,14 @@
         def _():
             here(acts, 3, act_recv)
 
-        @pl.when(r > 0)
-        def _():
-            project(page_of(r), 0)
-            project(page_of(r), 1)
-
-        dispatch(swap(page_of(r)))
-        dispatch(4 + swap(page_of(r)))
+        for j in range(2):
+
+            @pl.when(r > 0)
+            def _():
+                project(page_of(r), j)
+
+            dispatch(4 * j + swap(page_of(r)))
+
         return carry
 
     lax.fori_loop(0, 4, step, 0)
@@ -391,6 +394,10 @@
     here(weights, 1, w_recv)
     here(weights, 2, w_recv)
     weights_relay.start()
+    again = x_ref[...].astype(F32)
+    rms = lax.rsqrt(jnp.mean(again * again, axis=-1, keepdims=True) + 1e-05)
+    rms_kept[...] = rms
+    cubed[...] = again * rms**3
     total[...] = jnp.zeros_like(total)
     here(weights, 3, w_recv)
 
@@ -405,12 +412,9 @@
 
     lax.fori_loop(0, HALF, combine, 0)
 
-    again = x_ref[...].astype(F32)
-    rms = lax.rsqrt(jnp.mean(again * again, axis=-1, keepdims=True) + 1e-05)
     grad = total[...]
-    branch_out[...] = (
-        rms * grad - again * rms**3 * jnp.mean(grad * again, axis=-1, keepdims=True)
-    ).astype(BF16)
+    lean = jnp.mean(grad * x_ref[...].astype(F32), axis=-1, keepdims=True)
+    branch_out[...] = (rms_kept[...] * grad - cubed[...] * lean).astype(BF16)
     shift = pltpu.make_async_remote_copy(
         src_ref=branch_out,
         dst_ref=out_ref,
@@ -475,6 +479,8 @@
             pltpu.VMEM((HALF, H1, BLOCK), BF16),
             pltpu.VMEM((HALF, H2, BLOCK), BF16),
             pltpu.VMEM((BLOCK, WIDTH), F32),
+            pltpu.VMEM((BLOCK, 1), F32),
+            pltpu.VMEM((BLOCK, WIDTH), F32),
             pltpu.VMEM((BLOCK, WIDTH), BF16),
             dma((6,)),
             dma((3,)),

time: 98.1 us -> 98 us (level)
  no operation moved by 1% of the time
where the time goes in v6:
time: 98 us; the launch traced here: 97.8 us
  Pallas kernels  96.4 us (98%)
  local copies, waits for them, and re-layouts  1.41 us (1%)
    pallas_call x1, Pallas kernels, body(): pl.pallas_call(kernel, out_shape=jax.ShapeDtypeStruct((tokens, WIDTH), BF...  96.4 us

profile of v6, /device:TPU:157, one launch (start us, length us, event | category | flops | bytes accessed | tf_op | source)
XLA Modules:
  0.0 97.8 jit_solution(7254675551001656872)
XLA Ops:
  0.0 0.0 copy-start
  0.0 0.7 copy-done
  0.7 96.4 %shard_map.73 = bf16[128,1280]{1,0:T(8,128)(2,1)S(1)} custom-call(s32[4,16]{1,0:T(4,128)S(1)} %copy-done, bf16[128,1280]{1,0:T(8,128)(2,1)} %bitcast.24, bf16[128,1280]{1,0:T(8,128)(2,1)} %bitcast.25, bf16[2,80,1280]{2,1,0:T(8,128)(2,1)} %bitcast.20, bf16[2,80,1280]{2,1,0:T(8,128)(2,1)} %bitcast.21, bf16[2,80,1280]{2,1,0:T(8,128)(2,1)} %bitcast.22, ...), custom_call_target="tpu_custom_call" | custom-call | tf_op jit(solution)/shard_map/pallas_call | solution.py:460
  97.1 0.7 copy.9
Async XLA Ops:
  0.0 0.7 copy-start
